TPU v7x, 32 devices: a whole 2x2x4 slice. The times are simulated.
32 devices in a mesh: fsdp: 16 (over z, y, x), tp: 2 (over core).
Axes of the slice: x: 2, y: 2, z: 4, core: 2. Of those that a mesh axis runs over, the one named last changes fastest.
Arguments:
- tokens: bfloat16 [2, 2048, 8192], P(None, 'fsdp', 'tp'), may hold values from -6 to 6
- frozen_weight: bfloat16 [8192, 2048], P('tp', 'fsdp'), may hold values from -0.0625 to 0.0625
- cotangent: bfloat16 [2, 2048, 2048], P(None, 'fsdp'), may hold values from -6 to 6
- block_adapter_index: int32 [2, 16], replicated, may hold values from 0 to 511
- down_weight: bfloat16 [512, 8192, 16], P(None, ('tp', 'fsdp')), may hold values from -0.0625 to 0.0625
- up_weight: bfloat16 [512, 16, 2048], P(None, None, ('tp', 'fsdp')), may hold values from -0.125 to 0.125
Outputs:
- key_value_output: bfloat16 [2, 2048, 2048], P(None, 'fsdp', 'tp')
- input_gradient: bfloat16 [2, 2048, 8192], P(None, 'fsdp', 'tp')
- grad_down: float32 [512, 8192, 16], P(None, ('tp', 'fsdp'))
- up_weight_gradient: float32 [512, 16, 2048], P(None, None, ('tp', 'fsdp'))
Inputs may be any that keep to these rules, and one draw needn't show every extreme that they name: `block_adapter_index`: one adapter for each block of 128 rows of a microbatch.
All inputs are finite; a program needn't handle non-finite values.
Results may differ from a plain program's by a relative error of at most 0.005.
Values may be sent and summed in bfloat16 or wider, within the bound.
No kernel may reach another device: no remote copies, remote signals or barrier semaphores. Data moves between devices by JAX's collectives and lax.ppermute only.
A program may use at most 128 MiB of HBM per device.

v0:
```python
import jax
import jax.numpy as jnp
from jax import lax
from jax.sharding import PartitionSpec as P

BLOCK = 128
adapter_scale = 2.0


def selected_sum(adapter_selector, tiles):
    flat = tiles.reshape(tiles.shape[0], -1)
    return lax.dot_general(
        adapter_selector,
        flat,
        (((0,), (0,)), ((), ())),
        precision=lax.Precision.HIGHEST,
        preferred_element_type=jnp.float32,
    )


def local(tokens, frozen_weight, cotangent, block_adapter_index, down_weight, up_weight):
    microbatch_list, token_block_rows, shard_width = tokens.shape
    kv_width = cotangent.shape[2]
    key_value_slice = kv_width // lax.axis_size("tp")
    row_total = microbatch_list * token_block_rows
    tok_matrix = tokens.reshape(row_total, shard_width)
    cot_matrix = cotangent.reshape(row_total, kv_width)
    adapter_number = down_weight.shape[0]
    rank_width = down_weight.shape[2]
    adapter_range = jnp.arange(adapter_number, dtype=jnp.int32)
    gathered = lax.all_gather(frozen_weight, "fsdp", axis=1, tiled=True)
    kv_partial = jnp.dot(tok_matrix, gathered, preferred_element_type=jnp.float32)
    frozen_key_value = lax.psum_scatter(kv_partial, "tp", scatter_dimension=1, tiled=True)
    frozen_input_gradient = lax.dot_general(
        cot_matrix, gathered, (((1,), (1,)), ((), ())), preferred_element_type=jnp.float32
    )
    cot_slab = lax.dynamic_slice_in_dim(
        cotangent, lax.axis_index("tp") * key_value_slice, key_value_slice, 2
    )
    fsdp_count = lax.axis_size("fsdp")
    per_dev = token_block_rows // BLOCK
    dest_ids = (
        block_adapter_index.reshape(microbatch_list, fsdp_count, per_dev)
        .transpose(1, 0, 2)
        .reshape(fsdp_count, microbatch_list * per_dev)
    )
    down_send = jnp.take(down_weight, dest_ids, axis=0).transpose(0, 1, 3, 2)
    up_send = jnp.take(up_weight, dest_ids, axis=0)
    down_mine, up_mine = (
        lax.all_to_all(down_send, "fsdp", split_axis=0, concat_axis=3, tiled=True),
        lax.all_to_all(up_send, "fsdp", split_axis=0, concat_axis=3, tiled=True),
    )
    down_mine = down_mine.reshape(microbatch_list, per_dev, rank_width, shard_width)
    up_mine = up_mine.reshape(microbatch_list, per_dev, rank_width, key_value_slice)
    tok_blocks = tokens.reshape(microbatch_list, per_dev, BLOCK, shard_width)
    gradient_blocks = cot_slab.reshape(microbatch_list, per_dev, BLOCK, key_value_slice)
    low_part = jnp.einsum(
        "mnbc,mnrc->mnbr", tok_blocks, down_mine, preferred_element_type=jnp.float32
    )
    partial_input_gradient = adapter_scale * jnp.einsum(
        "fsvj,fsyj->fsvy", gradient_blocks, up_mine, preferred_element_type=jnp.float32
    )
    low_sum, back_sum = lax.psum((low_part, partial_input_gradient), "tp")
    low_rank = low_sum.astype(jnp.bfloat16)
    rank_gradient = back_sum.astype(jnp.bfloat16)
    adapter_key_value = (
        adapter_scale
        * jnp.einsum("elui,elis->elus", low_rank, up_mine, preferred_element_type=jnp.float32)
    ).astype(jnp.bfloat16)
    adapter_input_gradient = jnp.einsum(
        "mnbr,mnrc->mnbc", rank_gradient, down_mine, preferred_element_type=jnp.float32
    ).astype(jnp.bfloat16)
    adapter_key_value = adapter_key_value.reshape(
        microbatch_list, token_block_rows, key_value_slice
    )
    adapter_input_gradient = adapter_input_gradient.reshape(
        microbatch_list, token_block_rows, shard_width
    )
    down_tiles = jnp.einsum(
        "mnbc,mnbr->mnrc", tok_blocks, rank_gradient, preferred_element_type=jnp.float32
    )
    up_weight_tiles = adapter_scale * jnp.einsum(
        "puai,puac->puic", low_rank, gradient_blocks, preferred_element_type=jnp.float32
    )
    down_tiles = down_tiles.reshape(microbatch_list * per_dev, rank_width, shard_width)
    up_weight_tiles = up_weight_tiles.reshape(
        microbatch_list * per_dev, rank_width, key_value_slice
    )
    down_owned, up_owned = (
        lax.all_to_all(
            down_tiles.astype(jnp.bfloat16), "fsdp", split_axis=2, concat_axis=0, tiled=True
        ).astype(down_tiles.dtype),
        lax.all_to_all(
            up_weight_tiles.astype(jnp.bfloat16), "fsdp", split_axis=2, concat_axis=0, tiled=True
        ).astype(up_weight_tiles.dtype),
    )
    owned_ids = dest_ids.reshape(-1)
    adapter_selector = (owned_ids[:, None] == adapter_range[None, :]).astype(jnp.float32)
    grad_down = (
        selected_sum(adapter_selector, down_owned)
        .reshape(adapter_number, rank_width, down_weight.shape[1])
        .transpose(0, 2, 1)
    )
    up_weight_gradient = selected_sum(adapter_selector, up_owned).reshape(up_weight.shape)
    key_value_output = (
        frozen_key_value.reshape(microbatch_list, token_block_rows, key_value_slice)
        + adapter_key_value.astype(jnp.float32)
    ).astype(jnp.bfloat16)
    input_gradient = (
        frozen_input_gradient.reshape(microbatch_list, token_block_rows, shard_width)
        + adapter_input_gradient.astype(jnp.float32)
    ).astype(jnp.bfloat16)
    return (key_value_output, input_gradient, grad_down, up_weight_gradient)


def solution(mesh):
    return jax.shard_map(
        local,
        mesh=mesh,
        in_specs=(
            P(None, "fsdp", "tp"),
            P("tp", "fsdp"),
            P(None, "fsdp", None),
            P(),
            P(None, ("tp", "fsdp"), None),
            P(None, None, ("tp", "fsdp")),
        ),
        out_specs=(
            P(None, "fsdp", "tp"),
            P(None, "fsdp", "tp"),
            P(None, ("tp", "fsdp"), None),
            P(None, None, ("tp", "fsdp")),
        ),
        check_vma=False,
    )
```

profile of v0, /device:TPU:0, one launch (start us, length us, event | category | flops | bytes accessed | tf_op | source)
XLA Modules:
  0.0 380.9 jit_solution(13523982944340229810)
XLA Ops:
  8.0 3.8 copy.30
  12.1 2.2 gather_fusion.1
  14.3 248.3 %all-gather.2.cloned.1.call-done = bf16[4096,2048]{1,0:T(8,128)(2,1)} async-done(((bf16[4096,128]{1,0:T(8,128)(2,1)}), bf16[4096,2048]{1,0:T(8,128)(2,1)}) %all-gather.2.cloned.1.call-update) | async-done | bytes 16777232 | tf_op jit(solution)/shard_map/all_gather | solution.py:31
  262.6 9.5 %fusion.36 = f32[256,2048]{1,0:T(8,128)} fusion(bf16[256,4096]{1,0:T(8,128)(2,1)S(1)} %bitcast.91, bf16[4096,2048]{1,0:T(8,128)(2,1)} %all-gather.2.cloned.1.call-done), kind=kOutput, calls=%fused_computation.46 | convolution fusion | flops 4294967296 | bytes 20971520 | tf_op jit(solution)/shard_map/dot_general | solution.py:32
  272.9 3.8 all-to-all-start.1
  276.7 2.9 gather_fusion
  280.5 3.8 all-to-all-done.1
  284.3 3.5 all-to-all-start
  291.5 5.3 %all-to-all-done = bf16[16,2,16,256]{3,2,1,0:T(8,128)(2,1)S(1)} async-done(((bf16[16,2,16,256]{3,2,1,0:T(8,128)(2,1)}), bf16[16,2,16,256]{3,2,1,0:T(8,128)(2,1)S(1)}, u32[]{:S(2)}, u32[]{:S(2)}) %all-to-all-start) | async-done | bytes 262176 | tf_op jit(solution)/shard_map/all_to_all | solution.py:50
  299.4 3.4 all-reduce
  303.4 1.2 reshape.125
  304.6 3.5 all-to-all-start.3
  308.5 3.8 copy.33
  312.3 7.3 %reshape.123 = bf16[16,2,4096]{2,1,0:T(2,128)(2,1)} reshape(bf16[4096,2,16]{2,1,0:T(2,128)(2,1)} %bitcast.93) | data formatting | bytes 524288
  319.7 6.9 %all-to-all-start.2 = ((bf16[16,2,4096]{2,1,0:T(2,128)(2,1)}), bf16[16,2,4096]{2,1,0:T(2,128)(2,1)S(1)}, u32[]{:S(2)}, u32[]{:S(2)}) async-start(bf16[16,2,4096]{2,1,0:T(2,128)(2,1)} %reshape.123), calls=%async_computation.3 | async-start | bytes 524288 | tf_op jit(solution)/shard_map/all_to_all | solution.py:90
  326.6 2.7 fusion.5
  330.3 1.8 fusion.19
  332.2 4.5 %all-to-all-done.2 = bf16[16,2,4096]{2,1,0:T(2,128)(2,1)S(1)} async-done(((bf16[16,2,4096]{2,1,0:T(2,128)(2,1)}), bf16[16,2,4096]{2,1,0:T(2,128)(2,1)S(1)}, u32[]{:S(2)}, u32[]{:S(2)}) %all-to-all-start.2) | async-done | bytes 262176 | tf_op jit(solution)/shard_map/all_to_all | solution.py:90
  336.6 2.4 reshape.124
  339.0 4.4 %copy.34 = bf16[2,16,16,256]{3,1,0,2:T(8,128)(2,1)S(1)} copy(bf16[2,16,16,256]{1,0,3,2:T(2,128)(2,1)} %bitcast.94) | data formatting | bytes 524288 | tf_op jit(solution)/shard_map/all_to_all | solution.py:90
  343.4 1.4 convolution_bitcast_fusion
  344.8 8.3 %copy.39 = f32[512,256,16]{1,2,0:T(8,128)} copy(f32[512,256,16]{1,0,2:T(8,128)S(1)} %convolution_bitcast_fusion) | data formatting | bytes 16777216
  353.1 18.7 %fusion.6 = bf16[2,128,4096]{2,1,0:T(8,128)(2,1)} fusion(f32[2,128,4096]{2,1,0:T(8,128)} %fusion.5, bf16[2,128,2048]{2,1,0:T(8,128)(2,1)S(1)} %copy-done.2, bf16[4096,2048]{1,0:T(8,128)(2,1)} %all-gather.2.cloned.1.call-done), kind=kOutput, calls=%fused_computation.7 | convolution fusion | flops 4297064448 | bytes 24117248 | tf_op jit(solution)/shard_map/dot_general | solution.py:34
  371.7 2.4 fusion.12
  (43 shorter events, 11.0 us)
Async XLA Ops:
  7.2 255.4 %copy-start = (bf16[2,128,4096]{2,1,0:T(8,128)(2,1)S(1)}, bf16[2,128,4096]{2,1,0:T(8,128)(2,1)}, u32[]{:S(2)}) copy-start(bf16[2,128,4096]{2,1,0:T(8,128)(2,1)} %param.6) | copy-start | bytes 6291460
  7.2 4.6 %copy-start.5 = (s32[2,16]{1,0:T(2,128)S(1)}, s32[2,16]{1,0:T(2,128)}, u32[]{:S(2)}) copy-start(s32[2,16]{1,0:T(2,128)} %param.9) | copy-start | bytes 388
  7.2 255.4 %all-gather.2.cloned.1.call-start = ((), (), s32[]{:S(2)}) async-start(), calls=%async_computation.5 | async-start | bytes 17825792 | tf_op jit(solution)/shard_map/all_gather | solution.py:31
  7.9 363.8 %reduce-scatter.2.cloned.1.call-start = ((), (), s32[]{:S(2)}) async-start(), calls=%async_computation.6 | async-start | bytes 3145728 | tf_op jit(solution)/shard_map/reduce_scatter | solution.py:33
  272.9 11.3 %all-to-all-start.1 = ((bf16[16,2,1024]{2,1,0:T(2,128)(2,1)}), bf16[16,2,1024]{2,1,0:T(2,128)(2,1)S(1)}, u32[]{:S(2)}, u32[]{:S(2)}) async-start(bf16[16,2,1024]{2,1,0:T(2,128)(2,1)} %reshape.121), calls=%async_computation.2 | async-start | bytes 131072 | tf_op jit(solution)/shard_map/all_to_all | solution.py:51
  276.7 14.5 %copy-start.1 = (bf16[2,128,2048]{2,1,0:T(8,128)(2,1)S(1)}, bf16[2,128,2048]{2,1,0:T(8,128)(2,1)}, u32[]{:S(2)}) copy-start(bf16[2,128,2048]{2,1,0:T(8,128)(2,1)} %param.8) | copy-start | bytes 3145732
  284.3 4.2 %copy-start.3 = (bf16[16,2,1024]{2,1,0:T(2,128)(2,1)}, bf16[16,2,1024]{2,1,0:T(2,128)(2,1)S(1)}, u32[]{:S(2)}) copy-start(bf16[16,2,1024]{2,1,0:T(2,128)(2,1)S(1)} %all-to-all-done.1) | copy-start | bytes 196612
  284.3 12.6 %all-to-all-start = ((bf16[16,2,16,256]{3,2,1,0:T(8,128)(2,1)}), bf16[16,2,16,256]{3,2,1,0:T(8,128)(2,1)S(1)}, u32[]{:S(2)}, u32[]{:S(2)}) async-start(bf16[16,2,16,256]{3,2,1,0:T(8,128)(2,1)} %select_bitcast_fusion), calls=%async_computation.1 | async-start | bytes 524288 | tf_op jit(solution)/shard_map/all_to_all | solution.py:50
  304.6 15.1 %all-to-all-start.3 = ((bf16[16,2,1024]{2,1,0:T(2,128)(2,1)}), bf16[16,2,1024]{2,1,0:T(2,128)(2,1)S(1)}, u32[]{:S(2)}, u32[]{:S(2)}) async-start(bf16[16,2,1024]{2,1,0:T(2,128)(2,1)} %reshape.125), calls=%async_computation.4 | async-start | bytes 131072 | tf_op jit(solution)/shard_map/all_to_all | solution.py:93
  319.7 16.9 %all-to-all-start.2 = ((bf16[16,2,4096]{2,1,0:T(2,128)(2,1)}), bf16[16,2,4096]{2,1,0:T(2,128)(2,1)S(1)}, u32[]{:S(2)}, u32[]{:S(2)}) async-start(bf16[16,2,4096]{2,1,0:T(2,128)(2,1)} %reshape.123), calls=%async_computation.3 | async-start | bytes 524288 | tf_op jit(solution)/shard_map/all_to_all | solution.py:90
  326.6 3.7 copy-start.4
  344.8 8.3 %copy-start.2 = (bf16[2,128,2048]{2,1,0:T(8,128)(2,1)S(1)}, bf16[2,128,2048]{2,1,0:T(8,128)(2,1)}, u32[]{:S(2)}) copy-start(bf16[2,128,2048]{2,1,0:T(8,128)(2,1)} %param.8) | copy-start | bytes 3145732
Sparse Core Ops, SparseCore 0:
  10.7 251.8 all-gather.1
  272.2 7.8 reduce-scatter.1
where the time goes:
time: 382 us; the launch traced here: 381 us
  waiting for transfers between devices  263 us (69%)
  local copies, waits for them, and re-layouts  44.1 us (12%)
  matrix products  37.8 us (10%)
  starting transfers between devices  17.9 us (5%)
  between operations  14.2 us (4%)
    all_gather x1, waiting for transfers between devices, local(): gathered = lax.all_gather(frozen_weight, 'fsdp', axis=1, tiled=True)  248 us
    unnamed x20, local copies, waits for them, and re-layouts  25.1 us
    dot_general x1, matrix products, local(): lax.dot_general(cot_matrix, gathered, (((1,), (1,)), ((), ())), preferred...  18.7 us
    dot_general x1, matrix products, local(): jnp.dot(tok_matrix, gathered, preferred_element_type=jnp.float32)  9.45 us
  transfers between devices with their start and end apart: 6, of which 4 were waited for; matrix products, arithmetic and copies ran while one was open for 19% of the time, Pallas kernels for 0%

commit v1 on v0

--- a/solution.py
+++ b/solution.py
@@ -28,7 +28,7 @@
     adapter_number = down_weight.shape[0]
     rank_width = down_weight.shape[2]
     adapter_range = jnp.arange(adapter_number, dtype=jnp.int32)
-    gathered = lax.all_gather(frozen_weight, "fsdp", axis=1, tiled=True)
+    gathered = jnp.concatenate(lax.all_gather(frozen_weight, "fsdp"), axis=1)
     kv_partial = jnp.dot(tok_matrix, gathered, preferred_element_type=jnp.float32)
     frozen_key_value = lax.psum_scatter(kv_partial, "tp", scatter_dimension=1, tiled=True)
     frozen_input_gradient = lax.dot_general(

time: 382 us -> 361 us (0.945)
  waiting for transfers between devices: 263 us -> 206 us
  local copies, waits for them, and re-layouts: 44.1 us -> 78.1 us
    all_gather x1, waiting for transfers between devices: 248 us -> 190 us  [local(): gathered = jnp.concatenate(lax.all_gather(frozen_weight, 'fsdp'), axis=1)]
    reshape x0 -> x1, local copies, waits for them, and re-layouts: none -> 25.4 us  [local(): gathered = jnp.concatenate(lax.all_gather(frozen_weight, 'fsdp'), axis=1)]
    all_gather x0 -> x1, local copies, waits for them, and re-layouts: none -> 18.5 us  [local(): gathered = jnp.concatenate(lax.all_gather(frozen_weight, 'fsdp'), axis=1)]
    unnamed x20 -> x22, local copies, waits for them, and re-layouts: 25.1 us -> 19.6 us
  transfers between devices with their start and end apart: 6 -> 6, of which waited for: 4 -> 5; matrix products, arithmetic and copies ran while one was open for 19% -> 24% of each run, Pallas kernels for 0% -> 0%
where the time goes in v1:
time: 361 us; the launch traced here: 359 us
  waiting for transfers between devices  206 us (57%)
  local copies, waits for them, and re-layouts  78.1 us (22%)
  matrix products  40.4 us (11%)
  starting transfers between devices  16.4 us (5%)
  between operations  14.2 us (4%)
    all_gather x1, waiting for transfers between devices, local(): gathered = jnp.concatenate(lax.all_gather(frozen_weight, 'fsdp'), axis=1)  190 us
    reshape x1, local copies, waits for them, and re-layouts, local(): gathered = jnp.concatenate(lax.all_gather(frozen_weight, 'fsdp'), axis=1)  25.4 us
    unnamed x22, local copies, waits for them, and re-layouts  19.6 us
    dot_general x1, matrix products, local(): lax.dot_general(cot_matrix, gathered, (((1,), (1,)), ((), ())), preferred...  19 us
    all_gather x1, local copies, waits for them, and re-layouts, local(): gathered = jnp.concatenate(lax.all_gather(frozen_weight, 'fsdp'), axis=1)  18.5 us
    dot_general x1, matrix products, local(): jnp.dot(tok_matrix, gathered, preferred_element_type=jnp.float32)  11.6 us
  transfers between devices with their start and end apart: 6, of which 5 were waited for; matrix products, arithmetic and copies ran while one was open for 24% of the time, Pallas kernels for 0%

profile of v1, /device:TPU:0, one launch (start us, length us, event | category | flops | bytes accessed | tf_op | source)
XLA Modules:
  0.0 359.4 jit_solution(14652404561405023167)
XLA Ops:
  8.0 3.8 %copy.33 = bf16[512,16,64]{2,1,0:T(8,128)(2,1)} copy(bf16[512,16,64]{0,2,1:T(8,128)(2,1)} %param.11) | data formatting | bytes 2097152 | tf_op args[5]
  12.1 2.2 gather_fusion.1
  14.3 190.3 %all-gather.3.cloned.1.call-done = bf16[65536,128]{1,0:T(8,128)(2,1)} async-done(((bf16[4096,128]{1,0:T(8,128)(2,1)}), bf16[65536,128]{1,0:T(8,128)(2,1)}) %all-gather.3.cloned.1.call-update) | async-done | bytes 16777232 | tf_op jit(solution)/shard_map/all_gather | solution.py:31
  204.5 18.5 %copy.61 = bf16[16,4096,128]{2,0,1:T(8,128)(2,1)} copy(bf16[16,4096,128]{2,1,0:T(8,128)(2,1)} %bitcast.96) | data formatting | bytes 33554432 | tf_op jit(solution)/shard_map/all_gather | solution.py:31
  223.1 11.6 %fusion = f32[256,2048]{1,0:T(8,128)} fusion(bf16[256,4096]{1,0:T(8,128)(2,1)S(1)} %bitcast.92, bf16[512,8,16,128]{3,2,1,0:T(8,128)(2,1)} %bitcast.93), kind=kOutput, calls=%fused_computation.2 | convolution fusion | flops 4294967296 | bytes 20971520 | tf_op jit(solution)/shard_map/dot_general | solution.py:32
  235.6 3.8 %all-to-all-start.1 = ((bf16[16,2,1024]{2,1,0:T(2,128)(2,1)}), bf16[16,2,1024]{2,1,0:T(2,128)(2,1)S(1)}, u32[]{:S(2)}, u32[]{:S(2)}) async-start(bf16[16,2,1024]{2,1,0:T(2,128)(2,1)} %reshape.131), calls=%async_computation.2 | async-start | bytes 131072 | tf_op jit(solution)/shard_map/all_to_all | solution.py:51
  239.4 2.9 gather_fusion
  243.2 3.8 %all-to-all-done.1 = bf16[16,2,1024]{2,1,0:T(2,128)(2,1)S(1)} async-done(((bf16[16,2,1024]{2,1,0:T(2,128)(2,1)}), bf16[16,2,1024]{2,1,0:T(2,128)(2,1)S(1)}, u32[]{:S(2)}, u32[]{:S(2)}) %all-to-all-start.1) | async-done | bytes 65568 | tf_op jit(solution)/shard_map/all_to_all | solution.py:51
  246.9 3.5 all-to-all-start
  254.2 5.3 %all-to-all-done = bf16[16,2,16,256]{3,2,1,0:T(8,128)(2,1)S(1)} async-done(((bf16[16,2,16,256]{3,2,1,0:T(8,128)(2,1)}), bf16[16,2,16,256]{3,2,1,0:T(8,128)(2,1)S(1)}, u32[]{:S(2)}, u32[]{:S(2)}) %all-to-all-start) | async-done | bytes 262176 | tf_op jit(solution)/shard_map/all_to_all | solution.py:50
  262.1 3.4 all-reduce
  267.3 3.7 %all-to-all-start.3 = ((bf16[16,2,1024]{2,1,0:T(2,128)(2,1)}), bf16[16,2,1024]{2,1,0:T(2,128)(2,1)S(1)}, u32[]{:S(2)}, u32[]{:S(2)}) async-start(bf16[16,2,1024]{2,1,0:T(2,128)(2,1)} %reshape.135), calls=%async_computation.4 | async-start | bytes 131072 | tf_op jit(solution)/shard_map/all_to_all | solution.py:93
  271.3 2.7 copy.36
  274.1 2.8 reshape.133
  276.9 1.5 all-to-all-done.3
  278.3 5.3 %all-to-all-start.2 = ((bf16[16,2,4096]{2,1,0:T(2,128)(2,1)}), bf16[16,2,4096]{2,1,0:T(2,128)(2,1)S(1)}, u32[]{:S(2)}, u32[]{:S(2)}) async-start(bf16[16,2,4096]{2,1,0:T(2,128)(2,1)} %reshape.133), calls=%async_computation.3 | async-start | bytes 524288 | tf_op jit(solution)/shard_map/all_to_all | solution.py:90
  283.7 2.8 fusion.4
  287.5 1.8 fusion.15
  289.3 4.4 %all-to-all-done.2 = bf16[16,2,4096]{2,1,0:T(2,128)(2,1)S(1)} async-done(((bf16[16,2,4096]{2,1,0:T(2,128)(2,1)}), bf16[16,2,4096]{2,1,0:T(2,128)(2,1)S(1)}, u32[]{:S(2)}, u32[]{:S(2)}) %all-to-all-start.2) | async-done | bytes 262176 | tf_op jit(solution)/shard_map/all_to_all | solution.py:90
  293.7 1.4 reshape.134
  297.6 8.3 %copy.42 = f32[512,256,16]{1,2,0:T(8,128)} copy(f32[512,256,16]{1,0,2:T(8,128)S(1)} %convolution_bitcast_fusion) | data formatting | bytes 16777216
  305.8 25.4 %reshape.128 = bf16[4096,2048,1]{1,0,2:T(8,128)(2,1)} reshape(bf16[4096,16,128]{2,1,0:T(8,128)(2,1)} %bitcast.94) | data formatting | bytes 33554432 | tf_op jit(solution)/shard_map/reshape | solution.py:31
  331.2 19.0 %fusion.3 = bf16[2,128,4096]{2,1,0:T(8,128)(2,1)} fusion(f32[2,128,4096]{2,1,0:T(8,128)} %fusion.4, bf16[2,128,2048]{2,1,0:T(8,128)(2,1)S(1)} %copy-done.3, bf16[4096,2048,1]{1,0,2:T(8,128)(2,1)} %reshape.128), kind=kOutput, calls=%fused_computation.6 | convolution fusion | flops 4297064448 | bytes 24117248 | tf_op jit(solution)/shard_map/dot_general | solution.py:34
  350.2 2.4 fusion.8
  (47 shorter events, 14.6 us)
Async XLA Ops:
  7.2 215.9 %copy-start = (bf16[2,128,4096]{2,1,0:T(8,128)(2,1)S(1)}, bf16[2,128,4096]{2,1,0:T(8,128)(2,1)}, u32[]{:S(2)}) copy-start(bf16[2,128,4096]{2,1,0:T(8,128)(2,1)} %param.6) | copy-start | bytes 6291460
  7.2 4.6 %copy-start.6 = (s32[2,16]{1,0:T(2,128)S(1)}, s32[2,16]{1,0:T(2,128)}, u32[]{:S(2)}) copy-start(s32[2,16]{1,0:T(2,128)} %param.9) | copy-start | bytes 388
  7.2 197.3 %all-gather.3.cloned.1.call-start = ((), (), s32[]{:S(2)}) async-start(), calls=%async_computation.6 | async-start | bytes 17825792 | tf_op jit(solution)/shard_map/all_gather | solution.py:31
  7.9 342.3 %reduce-scatter.2.cloned.1.call-start = ((), (), s32[]{:S(2)}) async-start(), calls=%async_computation.5 | async-start | bytes 3145728 | tf_op jit(solution)/shard_map/reduce_scatter | solution.py:33
  235.6 11.3 %all-to-all-start.1 = ((bf16[16,2,1024]{2,1,0:T(2,128)(2,1)}), bf16[16,2,1024]{2,1,0:T(2,128)(2,1)S(1)}, u32[]{:S(2)}, u32[]{:S(2)}) async-start(bf16[16,2,1024]{2,1,0:T(2,128)(2,1)} %reshape.131), calls=%async_computation.2 | async-start | bytes 131072 | tf_op jit(solution)/shard_map/all_to_all | solution.py:51
  239.4 14.5 %copy-start.2 = (bf16[2,128,2048]{2,1,0:T(8,128)(2,1)S(1)}, bf16[2,128,2048]{2,1,0:T(8,128)(2,1)}, u32[]{:S(2)}) copy-start(bf16[2,128,2048]{2,1,0:T(8,128)(2,1)} %param.8) | copy-start | bytes 3145732
  246.9 4.2 %copy-start.4 = (bf16[16,2,1024]{2,1,0:T(2,128)(2,1)}, bf16[16,2,1024]{2,1,0:T(2,128)(2,1)S(1)}, u32[]{:S(2)}) copy-start(bf16[16,2,1024]{2,1,0:T(2,128)(2,1)S(1)} %all-to-all-done.1) | copy-start | bytes 196612
  246.9 12.6 %all-to-all-start = ((bf16[16,2,16,256]{3,2,1,0:T(8,128)(2,1)}), bf16[16,2,16,256]{3,2,1,0:T(8,128)(2,1)S(1)}, u32[]{:S(2)}, u32[]{:S(2)}) async-start(bf16[16,2,16,256]{3,2,1,0:T(8,128)(2,1)} %select_bitcast_fusion), calls=%async_computation.1 | async-start | bytes 524288 | tf_op jit(solution)/shard_map/all_to_all | solution.py:50
  267.3 11.1 %all-to-all-start.3 = ((bf16[16,2,1024]{2,1,0:T(2,128)(2,1)}), bf16[16,2,1024]{2,1,0:T(2,128)(2,1)S(1)}, u32[]{:S(2)}, u32[]{:S(2)}) async-start(bf16[16,2,1024]{2,1,0:T(2,128)(2,1)} %reshape.135), calls=%async_computation.4 | async-start | bytes 131072 | tf_op jit(solution)/shard_map/all_to_all | solution.py:93
  278.3 15.3 %all-to-all-start.2 = ((bf16[16,2,4096]{2,1,0:T(2,128)(2,1)}), bf16[16,2,4096]{2,1,0:T(2,128)(2,1)S(1)}, u32[]{:S(2)}, u32[]{:S(2)}) async-start(bf16[16,2,4096]{2,1,0:T(2,128)(2,1)} %reshape.133), calls=%async_computation.3 | async-start | bytes 524288 | tf_op jit(solution)/shard_map/all_to_all | solution.py:90
  283.7 3.8 %copy-start.5 = (s32[32]{0:T(128)S(1)}, s32[32]{0:T(128)}, u32[]{:S(2)}) copy-start(s32[32]{0:T(128)} %eq.15) | copy-start | bytes 388
  305.8 25.4 %copy-start.3 = (bf16[2,128,2048]{2,1,0:T(8,128)(2,1)S(1)}, bf16[2,128,2048]{2,1,0:T(8,128)(2,1)}, u32[]{:S(2)}) copy-start(bf16[2,128,2048]{2,1,0:T(8,128)(2,1)} %param.8) | copy-start | bytes 3145732
  331.2 21.4 %copy-start.1 = (bf16[2,128,4096]{2,1,0:T(8,128)(2,1)S(1)}, bf16[2,128,4096]{2,1,0:T(8,128)(2,1)}, u32[]{:S(2)}) copy-start(bf16[2,128,4096]{2,1,0:T(8,128)(2,1)} %param.6) | copy-start | bytes 6291460
Sparse Core Ops, SparseCore 0:
  10.8 193.7 all-gather.2
  234.8 7.8 reduce-scatter.1
